TPU v7x, 256 devices: a whole 4x4x8 slice. The times are simulated.
256 devices in a mesh: dp: 32 (over y, x, z_lo), mp: 8 (over z_hi, core).
Axes of the slice: x: 4, y: 4, z: 8 (z_hi: 4, z_lo: 2; z = z_hi * 2 + z_lo), core: 2. Of those that a mesh axis runs over, the one named last changes fastest.
Arguments:
- inputs: bfloat16 [4096, 16384], P('dp', 'mp'), may hold values from -6 to 6
- projector: bfloat16 [16384, 1024], P('dp', 'mp'), may hold values from -0.046875 to 0.046875
- out_grads: bfloat16 [4096, 26624], P('dp', 'mp'), may hold values from -0.25 to 0.25
- weights: bfloat16 [16384, 26624], P('dp', 'mp'), may hold values from -6 to 6
- first_moment: float32 [1024, 26624], P('dp', 'mp'), may hold values from -1.5 to 1.5
- second_moment: float32 [1024, 26624], P('dp', 'mp'), may hold values from 0.01 to 1
Outputs:
- new_weights: bfloat16 [16384, 26624], P('dp', 'mp')
- new_first: float32 [1024, 26624], P('dp', 'mp')
- new_second: float32 [1024, 26624], P('dp', 'mp')
All inputs are finite; a program needn't handle non-finite values.
Results may differ from a plain program's by a relative error of at most 0.0031.
Values may be sent and summed in bfloat16 or wider, within the bound.
A program may use at most 128 MiB of HBM per device.

v0:
```python
import jax
import jax.numpy as jnp
from jax import lax
from jax.sharding import Mesh
from jax.sharding import PartitionSpec as P

STEP = 1000
DP = ("dp_0", "dp_1", "dp_2")
MP = ("mp_0", "mp_1")


def joined_along(parts, dim):
    dims = list(parts.shape[1:])
    dims[dim] *= parts.shape[0]
    return jnp.moveaxis(parts, 0, dim).reshape(dims)


def copy_for_each(x, axis):
    peers = lax.axis_size(axis)
    return lax.all_to_all(jnp.broadcast_to(x[None], (peers, *x.shape)), axis, 0, 0, tiled=True)


def collect(x, axis, dim):
    return joined_along(copy_for_each(x, axis), dim)


def summed_rows(total, axes):
    for axis in axes:
        total = lax.psum_scatter(total, axis, scatter_dimension=0, tiled=True)
    return total


def stacked_from(x, axes, order):
    parts = x[None]
    for k in order:
        parts = lax.all_gather(parts, axes[k], axis=0, tiled=True)
    block = [lax.axis_size(axes[k]) for k in reversed(order)]
    parts = parts.reshape(*block, *x.shape)
    turned = sorted(range(len(order)), key=lambda place: order[len(order) - 1 - place])
    return parts.transpose(*turned, *range(len(order), parts.ndim)).reshape(-1, *x.shape)


def gather_axes(x, axes, order, dim):
    return joined_along(stacked_from(x, axes, order), dim)


def per_device(inputs, projector, out_grads, weights, first_moment, second_moment):
    columns = collect(projector, DP, 0)
    own_part = jnp.dot(
        lax.all_gather(inputs, MP, axis=1, tiled=True), columns, preferred_element_type=jnp.float32
    )
    projected = collect(own_part.astype(jnp.bfloat16), MP, 1)
    compressed = summed_rows(
        lax.dot_general(
            projected, out_grads, (((0,), (0,)), ((), ())), preferred_element_type=jnp.float32
        ),
        DP,
    )
    new_first = 0.9 * first_moment + 0.1 * compressed
    new_second = 0.999 * second_moment + 0.001 * compressed * compressed
    first_fix = 1.0 - 0.9**STEP
    second_fix = 1.0 - 0.999**STEP
    direction = (new_first / first_fix / (jnp.sqrt(new_second / second_fix) + 1e-08)).astype(
        jnp.bfloat16
    )
    full_rows = gather_axes(projector, MP, (0, 1), 1)
    empty = jnp.zeros(weights.shape, jnp.float32)
    piece = lax.all_gather(direction, DP, axis=0, tiled=True)
    ranks = lax.slice_in_dim(full_rows, 0, piece.shape[0], axis=1)
    lifted = empty + jnp.dot(ranks, piece, preferred_element_type=jnp.float32)
    new_weights = (weights.astype(jnp.float32) - 2.0 * lifted).astype(jnp.bfloat16)
    return (new_weights, new_first, new_second)


def solution(mesh):
    finer = Mesh(mesh.devices.reshape(4, 4, 2, 4, 2), ("dp_0", "dp_1", "dp_2", "mp_0", "mp_1"))
    in_specs = (P(DP, MP), P(DP, MP), P(DP, MP), P(DP, MP), P(DP, MP), P(DP, MP))
    out_specs = (P(DP, MP), P(DP, MP), P(DP, MP))
    return jax.shard_map(
        per_device, mesh=finer, in_specs=in_specs, out_specs=out_specs, check_vma=False
    )
```

profile of v0, /device:TPU:64, one launch (start us, length us, event | category | flops | bytes accessed | tf_op | source)
XLA Modules:
  0.0 534.7 jit_solution(4391776235239729843)
XLA Ops:
  8.0 3.9 broadcast_in_dim.6
  11.9 8.8 %all-to-all-start = ((bf16[32,512,128]{2,1,0:T(8,128)(2,1)}), bf16[32,512,128]{2,1,0:T(8,128)(2,1)}, u32[]{:S(2)}, u32[]{:S(2)}) async-start(bf16[32,512,128]{2,1,0:T(8,128)(2,1)} %broadcast_in_dim.6), calls=%async_computation | async-start | bytes 8388608 | tf_op jit(solution)/shard_map/all_to_all | solution.py:20
  20.7 0.0 all-gather.5.cloned.1.call-start
  20.8 0.7 all-gather.5.cloned.1.call-update
  21.5 69.8 %all-gather.5.cloned.1.call-done = bf16[128,16384]{1,0:T(8,128)(2,1)} async-done(((bf16[128,2048]{1,0:T(8,128)(2,1)}), bf16[128,16384]{1,0:T(8,128)(2,1)}) %all-gather.5.cloned.1.call-update) | async-done | bytes 4194320 | tf_op jit(solution)/shard_map/all_gather | solution.py:50
  91.3 14.7 %all-to-all-done = bf16[32,512,128]{2,1,0:T(8,128)(2,1)} async-done(((bf16[32,512,128]{2,1,0:T(8,128)(2,1)}), bf16[32,512,128]{2,1,0:T(8,128)(2,1)}, u32[]{:S(2)}, u32[]{:S(2)}) %all-to-all-start) | async-done | bytes 4194336 | tf_op jit(solution)/shard_map/all_to_all | solution.py:20
  106.0 4.7 convolution_convert_fusion
  110.7 0.1 copy.21
  110.9 17.4 %all_to_all.10 = bf16[8,128,128]{1,2,0:T(8,128)(2,1)S(1)} all-to-all(bf16[8,128,128]{1,2,0:T(8,128)(2,1)S(1)} %broadcast_in_dim.7), channel_id=1, replica_groups=mesh['dp_0'=4,'dp_1'=4,'dp_2'=2,'mp_0'=4,'mp_1'=2] {'mp_0','mp_1'}, dimensions={0} | all-to-all | bytes 524288 | tf_op jit(solution)/shard_map/all_to_all | solution.py:20
  128.3 6.8 %fusion.3 = f32[1024,3328]{1,0:T(8,128)} fusion(bf16[128,1024]{0,1:T(8,128)(2,1)S(1)} %bitcast.24, bf16[128,3328]{1,0:T(8,128)(2,1)S(1)} %copy-done), kind=kOutput, calls=%fused_computation.7 | convolution fusion | flops 872415232 | bytes 14745600 | tf_op jit(solution)/shard_map/dot_general | solution.py:54
  135.2 0.0 reduce-scatter.6.cloned.1.call-start
  135.2 119.8 %reduce-scatter.4.cloned.1.call-done = f32[256,3328]{1,0:T(8,128)} async-done(((f32[1024,3328]{1,0:T(8,128)}), f32[256,3328]{1,0:T(8,128)}) %reduce-scatter.4.cloned.1.call-update) | async-done | bytes 3407888 | tf_op jit(solution)/shard_map/reduce_scatter | solution.py:29
  255.1 45.2 %reduce-scatter.6.cloned.1.call-done = f32[64,3328]{1,0:T(8,128)} async-done(((f32[256,3328]{1,0:T(8,128)}), f32[64,3328]{1,0:T(8,128)}) %reduce-scatter.6.cloned.1.call-update) | async-done | bytes 851984 | tf_op jit(solution)/shard_map/reduce_scatter | solution.py:29
  300.3 0.0 all-gather.9.cloned.1.call-start
  300.4 18.8 %all-gather = bf16[2048,128]{1,0:T(8,128)(2,1)} all-gather(bf16[512,128]{1,0:T(8,128)(2,1)S(1)} %copy-done.1), channel_id=2, replica_groups=mesh['dp_0'=4,'dp_1'=4,'dp_2'=2,'mp_0'=4,'mp_1'=2] {'mp_0'}, dimensions={0}, use_global_device_ids=true | all-gather | bytes 655360 | tf_op jit(solution)/shard_map/all_gather | solution.py:36
  319.2 0.0 all-gather.7.cloned.1.call-start
  319.3 8.0 %reduce-scatter.8.cloned.1.call-done = f32[32,3328]{1,0:T(8,128)} async-done(((f32[64,3328]{1,0:T(8,128)}), f32[32,3328]{1,0:T(8,128)}) %reduce-scatter.8.cloned.1.call-update) | async-done | bytes 426000 | tf_op jit(solution)/shard_map/reduce_scatter | solution.py:29
  327.3 2.1 divide_convert_fusion
  329.4 5.6 %copy.20 = bf16[512,3328]{0,1:T(8,128)(2,1)} copy(bf16[512,3328]{1,0:T(8,128)(2,1)} %param.9) | data formatting | bytes 6815744 | tf_op args[3]
  335.1 1.3 copy.22
  336.4 0.5 copy.23
  336.9 176.4 %all-gather.7.cloned.1.call-done = bf16[1024,3328]{1,0:T(8,128)(2,1)} async-done(((bf16[32,3328]{1,0:T(8,128)(2,1)}), bf16[1024,3328]{1,0:T(8,128)(2,1)}) %all-gather.7.cloned.1.call-update) | async-done | bytes 6815760 | tf_op jit(solution)/shard_map/all_gather | solution.py:68
  513.3 8.7 %fusion = bf16[512,3328]{0,1:T(8,128)(2,1)} fusion(bf16[512,3328]{0,1:T(8,128)(2,1)} %copy.20, bf16[1024,3328]{1,0:T(8,128)(2,1)} %all-gather.7.cloned.1.call-done, bf16[512,1024]{0,1:T(8,128)(2,1)S(1)} %bitcast.26), kind=kOutput, calls=%fused_computation.1 | convolution fusion | flops 3496476672 | bytes 14680064 | tf_op jit(solution)/shard_map/dot_general | solution.py:70
  522.0 5.5 %copy.24 = bf16[512,3328]{1,0:T(8,128)(2,1)} copy(bf16[512,3328]{0,1:T(8,128)(2,1)} %fusion) | data formatting | bytes 6815744
  (17 shorter events, 0.2 us)
Async XLA Ops:
  8.0 120.3 %copy-start = (bf16[128,3328]{1,0:T(8,128)(2,1)S(1)}, bf16[128,3328]{1,0:T(8,128)(2,1)}, u32[]{:S(2)}) copy-start(bf16[128,3328]{1,0:T(8,128)(2,1)} %param.8) | copy-start | bytes 2555908
  11.9 94.1 %all-to-all-start = ((bf16[32,512,128]{2,1,0:T(8,128)(2,1)}), bf16[32,512,128]{2,1,0:T(8,128)(2,1)}, u32[]{:S(2)}, u32[]{:S(2)}) async-start(bf16[32,512,128]{2,1,0:T(8,128)(2,1)} %broadcast_in_dim.6), calls=%async_computation | async-start | bytes 8388608 | tf_op jit(solution)/shard_map/all_to_all | solution.py:20
  20.7 70.6 %all-gather.5.cloned.1.call-start = ((), (), s32[]{:S(2)}) async-start(), calls=%async_computation.5 | async-start | bytes 4718592 | tf_op jit(solution)/shard_map/all_gather | solution.py:50
  21.5 233.6 %reduce-scatter.4.cloned.1.call-start = ((), (), s32[]{:S(2)}) async-start(), calls=%async_computation.6 | async-start | bytes 17039360 | tf_op jit(solution)/shard_map/reduce_scatter | solution.py:29
  135.1 165.3 %copy-start.1 = (bf16[512,128]{1,0:T(8,128)(2,1)S(1)}, bf16[512,128]{1,0:T(8,128)(2,1)}, u32[]{:S(2)}) copy-start(bf16[512,128]{1,0:T(8,128)(2,1)} %param.7) | copy-start | bytes 393220
  135.2 192.2 %copy-start.2 = (f32[32,3328]{1,0:T(8,128)S(1)}, f32[32,3328]{1,0:T(8,128)}, u32[]{:S(2)}) copy-start(f32[32,3328]{1,0:T(8,128)} %param.11) | copy-start | bytes 1277956
  135.2 192.1 %copy-start.3 = (f32[32,3328]{1,0:T(8,128)S(1)}, f32[32,3328]{1,0:T(8,128)}, u32[]{:S(2)}) copy-start(f32[32,3328]{1,0:T(8,128)} %param.10) | copy-start | bytes 1277956
  135.2 165.1 %reduce-scatter.6.cloned.1.call-start = ((), (), s32[]{:S(2)}) async-start(), calls=%async_computation.7 | async-start | bytes 4259840 | tf_op jit(solution)/shard_map/reduce_scatter | solution.py:29
  255.1 72.2 %reduce-scatter.8.cloned.1.call-start = ((), (), s32[]{:S(2)}) async-start(), calls=%async_computation.8 | async-start | bytes 1277952 | tf_op jit(solution)/shard_map/reduce_scatter | solution.py:29
  300.3 34.7 %all-gather.9.cloned.1.call-start = ((), (), s32[]{:S(2)}) async-start(), calls=%async_computation.10 | async-start | bytes 1572864 | tf_op jit(solution)/shard_map/all_gather | solution.py:36
  319.2 194.1 %all-gather.7.cloned.1.call-start = ((), (), s32[]{:S(2)}) async-start(), calls=%async_computation.9 | async-start | bytes 7028736 | tf_op jit(solution)/shard_map/all_gather | solution.py:68
Sparse Core Ops, SparseCore 0:
  23.4 67.9 all-gather.4
  135.3 119.7 reduce-scatter.3
  257.6 42.6 reduce-scatter.5
  302.7 24.5 reduce-scatter.7
Sparse Core Ops, SparseCore 1:
  319.3 13.1 all-gather.8
  334.1 179.2 all-gather.6
where the time goes:
time: 535 us
  waiting for transfers between devices  435 us (81%)
  blocking collectives  36.1 us (7%)
  matrix products  20.3 us (4%)
  local copies, waits for them, and re-layouts  17.1 us (3%)
  between operations  15.3 us (3%)
  starting transfers between devices  9.05 us (2%)
    all_gather x1, waiting for transfers between devices, per_device(): piece = lax.all_gather(direction, DP, axis=0, tiled=True)  176 us
    reduce_scatter x3, waiting for transfers between devices, summed_rows(): total = lax.psum_scatter(total, axis, scatter_dimension=0, tiled=True)  173 us
    all_gather x1, waiting for transfers between devices, per_device(): lax.all_gather(inputs, MP, axis=1, tiled=True)  69.8 us
    all_gather x1, blocking collectives, stacked_from(): parts = lax.all_gather(parts, axes[k], axis=0, tiled=True)  18.8 us
    all_to_all x1, blocking collectives, copy_for_each(): lax.all_to_all(jnp.broadcast_to(x[None], (peers, *x.shape)), axis, 0, 0,...  17.4 us
    all_to_all x1, waiting for transfers between devices, copy_for_each(): lax.all_to_all(jnp.broadcast_to(x[None], (peers, *x.shape)), axis, 0, 0,...  14.7 us
    unnamed x10, local copies, waits for them, and re-layouts  11.2 us
  transfers between devices with their start and end apart: 7, of which 6 were waited for; matrix products, arithmetic and copies ran while one was open for 2% of the time, Pallas kernels for 0%

commit v1 on v0

--- a/solution.py
+++ b/solution.py
@@ -65,7 +65,8 @@
     )
     full_rows = gather_axes(projector, MP, (0, 1), 1)
     empty = jnp.zeros(weights.shape, jnp.float32)
-    piece = lax.all_gather(direction, DP, axis=0, tiled=True)
+    outgoing = jnp.stack([direction] * lax.axis_size(DP))
+    piece = jnp.concatenate(lax.all_to_all(outgoing, DP, 0, 0), axis=0)
     ranks = lax.slice_in_dim(full_rows, 0, piece.shape[0], axis=1)
     lifted = empty + jnp.dot(ranks, piece, preferred_element_type=jnp.float32)
     new_weights = (weights.astype(jnp.float32) - 2.0 * lifted).astype(jnp.bfloat16)

time: 535 us -> 497 us (0.929)
  waiting for transfers between devices: 435 us -> 293 us
  blocking collectives: 36.1 us -> 126 us
  starting transfers between devices: 9.05 us -> 16.3 us
    all_gather x1 -> x0, waiting for transfers between devices: 176 us -> none  [per_device(): piece = lax.all_gather(direction, DP, axis=0, tiled=True)]
    all_gather x1, blocking collectives: 18.8 us -> 109 us  [stacked_from(): parts = lax.all_gather(parts, axes[k], axis=0, tiled=True)]
    reduce_scatter x3, waiting for transfers between devices: 173 us -> 191 us  [summed_rows(): total = lax.psum_scatter(total, axis, scatter_dimension=0, tiled=True)]
    all_gather x1, waiting for transfers between devices: 0.01 us -> 17.4 us  [stacked_from(): parts = lax.all_gather(parts, axes[k], axis=0, tiled=True)]
    all_to_all x0 -> x1, starting transfers between devices: none -> 7.34 us  [per_device(): piece = jnp.concatenate(lax.all_to_all(outgoing, DP, 0, 0), axis=0)]
  transfers between devices with their start and end apart: 7 -> 7, of which waited for: 6 -> 6; matrix products, arithmetic and copies ran while one was open for 2% -> 1% of each run, Pallas kernels for 0% -> 0%
where the time goes in v1:
time: 497 us; the launch traced here: 494 us
  waiting for transfers between devices  293 us (59%)
  blocking collectives  126 us (25%)
  local copies, waits for them, and re-layouts  20.6 us (4%)
  matrix products  20.3 us (4%)
  starting transfers between devices  16.3 us (3%)
  between operations  15.3 us (3%)
    reduce_scatter x3, waiting for transfers between devices, summed_rows(): total = lax.psum_scatter(total, axis, scatter_dimension=0, tiled=True)  191 us
    all_gather x1, blocking collectives, stacked_from(): parts = lax.all_gather(parts, axes[k], axis=0, tiled=True)  109 us
    all_gather x1, waiting for transfers between devices, per_device(): lax.all_gather(inputs, MP, axis=1, tiled=True)  69.8 us
    all_gather x1, waiting for transfers between devices, stacked_from(): parts = lax.all_gather(parts, axes[k], axis=0, tiled=True)  17.4 us
    all_to_all x1, blocking collectives, copy_for_each(): lax.all_to_all(jnp.broadcast_to(x[None], (peers, *x.shape)), axis, 0, 0,...  17.4 us
    all_to_all x1, waiting for transfers between devices, copy_for_each(): lax.all_to_all(jnp.broadcast_to(x[None], (peers, *x.shape)), axis, 0, 0,...  14.7 us
    unnamed x10, local copies, waits for them, and re-layouts  11.1 us
  transfers between devices with their start and end apart: 7, of which 6 were waited for; matrix products, arithmetic and copies ran while one was open for 1% of the time, Pallas kernels for 0%

profile of v1, /device:TPU:64, one launch (start us, length us, event | category | flops | bytes accessed | tf_op | source)
XLA Modules:
  0.0 494.2 jit_solution(10229775811812718573)
XLA Ops:
  8.0 3.9 broadcast_in_dim.6
  11.9 8.8 %all-to-all-start = ((bf16[32,512,128]{2,1,0:T(8,128)(2,1)}), bf16[32,512,128]{2,1,0:T(8,128)(2,1)}, u32[]{:S(2)}, u32[]{:S(2)}) async-start(bf16[32,512,128]{2,1,0:T(8,128)(2,1)} %broadcast_in_dim.6), calls=%async_computation | async-start | bytes 8388608 | tf_op jit(solution)/shard_map/all_to_all | solution.py:20
  20.8 0.7 all-gather.4.cloned.1.call-update
  21.5 69.8 %all-gather.4.cloned.1.call-done = bf16[128,16384]{1,0:T(8,128)(2,1)} async-done(((bf16[128,2048]{1,0:T(8,128)(2,1)}), bf16[128,16384]{1,0:T(8,128)(2,1)}) %all-gather.4.cloned.1.call-update) | async-done | bytes 4194320 | tf_op jit(solution)/shard_map/all_gather | solution.py:50
  91.3 14.7 %all-to-all-done = bf16[32,512,128]{2,1,0:T(8,128)(2,1)} async-done(((bf16[32,512,128]{2,1,0:T(8,128)(2,1)}), bf16[32,512,128]{2,1,0:T(8,128)(2,1)}, u32[]{:S(2)}, u32[]{:S(2)}) %all-to-all-start) | async-done | bytes 4194336 | tf_op jit(solution)/shard_map/all_to_all | solution.py:20
  106.0 4.7 convolution_convert_fusion
  110.7 0.1 copy.21
  110.9 17.4 %all_to_all.15 = bf16[8,128,128]{1,2,0:T(8,128)(2,1)S(1)} all-to-all(bf16[8,128,128]{1,2,0:T(8,128)(2,1)S(1)} %broadcast_in_dim.7), channel_id=1, replica_groups=mesh['dp_0'=4,'dp_1'=4,'dp_2'=2,'mp_0'=4,'mp_1'=2] {'mp_0','mp_1'}, dimensions={0} | all-to-all | bytes 524288 | tf_op jit(solution)/shard_map/all_to_all | solution.py:20
  128.3 6.8 %fusion.3 = f32[1024,3328]{1,0:T(8,128)} fusion(bf16[128,1024]{0,1:T(8,128)(2,1)S(1)} %bitcast.25, bf16[128,3328]{1,0:T(8,128)(2,1)S(1)} %copy-done), kind=kOutput, calls=%fused_computation.7 | convolution fusion | flops 872415232 | bytes 14745600 | tf_op jit(solution)/shard_map/dot_general | solution.py:54
  135.2 0.0 reduce-scatter.6.cloned.1.call-start
  135.2 119.8 %reduce-scatter.4.cloned.1.call-done = f32[256,3328]{1,0:T(8,128)} async-done(((f32[1024,3328]{1,0:T(8,128)}), f32[256,3328]{1,0:T(8,128)}) %reduce-scatter.4.cloned.1.call-update) | async-done | bytes 3407888 | tf_op jit(solution)/shard_map/reduce_scatter | solution.py:29
  255.1 45.2 %reduce-scatter.6.cloned.1.call-done = f32[64,3328]{1,0:T(8,128)} async-done(((f32[256,3328]{1,0:T(8,128)}), f32[64,3328]{1,0:T(8,128)}) %reduce-scatter.6.cloned.1.call-update) | async-done | bytes 851984 | tf_op jit(solution)/shard_map/reduce_scatter | solution.py:29
  300.3 25.6 %reduce-scatter.8.cloned.1.call-done = f32[32,3328]{1,0:T(8,128)} async-done(((f32[64,3328]{1,0:T(8,128)}), f32[32,3328]{1,0:T(8,128)}) %reduce-scatter.8.cloned.1.call-update) | async-done | bytes 426000 | tf_op jit(solution)/shard_map/reduce_scatter | solution.py:29
  325.9 2.2 divide_convert_fusion
  328.1 3.7 stack.2
  331.7 7.3 %all-to-all-start.2 = ((bf16[32,32,3328]{2,1,0:T(8,128)(2,1)}), bf16[32,32,3328]{2,1,0:T(8,128)(2,1)}, u32[]{:S(2)}, u32[]{:S(2)}) async-start(bf16[32,32,3328]{2,1,0:T(8,128)(2,1)} %stack.2), calls=%async_computation.5 | async-start | bytes 13631488 | tf_op jit(solution)/shard_map/all_to_all | solution.py:69
  339.1 0.0 all-gather.6.cloned.1.call-start
  339.1 108.9 %all-gather = bf16[2048,128]{1,0:T(8,128)(2,1)} all-gather(bf16[512,128]{1,0:T(8,128)(2,1)S(1)} %copy-done.1), channel_id=2, replica_groups=mesh['dp_0'=4,'dp_1'=4,'dp_2'=2,'mp_0'=4,'mp_1'=2] {'mp_0'}, dimensions={0}, use_global_device_ids=true | all-gather | bytes 655360 | tf_op jit(solution)/shard_map/all_gather | solution.py:36
  448.0 5.6 %copy.20 = bf16[512,3328]{0,1:T(8,128)(2,1)} copy(bf16[512,3328]{1,0:T(8,128)(2,1)} %param.9) | data formatting | bytes 6815744 | tf_op args[3]
  453.6 17.4 %all-gather.6.cloned.1.call-done = bf16[8,512,128]{2,1,0:T(8,128)(2,1)} async-done(((bf16[4,512,128]{2,1,0:T(8,128)(2,1)}), bf16[8,512,128]{2,1,0:T(8,128)(2,1)}) %all-gather.6.cloned.1.call-update) | async-done | bytes 1048592 | tf_op jit(solution)/shard_map/all_gather | solution.py:36
  471.0 1.3 copy.22
  472.3 0.5 copy.23
  472.8 8.8 %fusion = bf16[512,3328]{0,1:T(8,128)(2,1)} fusion(bf16[512,3328]{0,1:T(8,128)(2,1)} %copy.20, bf16[1024,3328]{1,0:T(8,128)(2,1)} %bitcast.3, bf16[512,1024]{0,1:T(8,128)(2,1)S(1)} %bitcast.27), kind=kOutput, calls=%fused_computation.1 | convolution fusion | flops 3496476672 | bytes 14680064 | tf_op jit(solution)/shard_map/dot_general | solution.py:71
  481.6 5.5 %copy.24 = bf16[512,3328]{1,0:T(8,128)(2,1)} copy(bf16[512,3328]{0,1:T(8,128)(2,1)} %fusion) | data formatting | bytes 6815744
  (17 shorter events, 0.3 us)
Async XLA Ops:
  8.0 120.3 %copy-start = (bf16[128,3328]{1,0:T(8,128)(2,1)S(1)}, bf16[128,3328]{1,0:T(8,128)(2,1)}, u32[]{:S(2)}) copy-start(bf16[128,3328]{1,0:T(8,128)(2,1)} %param.8) | copy-start | bytes 2555908
  11.9 94.1 %all-to-all-start = ((bf16[32,512,128]{2,1,0:T(8,128)(2,1)}), bf16[32,512,128]{2,1,0:T(8,128)(2,1)}, u32[]{:S(2)}, u32[]{:S(2)}) async-start(bf16[32,512,128]{2,1,0:T(8,128)(2,1)} %broadcast_in_dim.6), calls=%async_computation | async-start | bytes 8388608 | tf_op jit(solution)/shard_map/all_to_all | solution.py:20
  20.7 70.6 %all-gather.4.cloned.1.call-start = ((), (), s32[]{:S(2)}) async-start(), calls=%async_computation.6 | async-start | bytes 4718592 | tf_op jit(solution)/shard_map/all_gather | solution.py:50
  21.4 233.6 %reduce-scatter.4.cloned.1.call-start = ((), (), s32[]{:S(2)}) async-start(), calls=%async_computation.7 | async-start | bytes 17039360 | tf_op jit(solution)/shard_map/reduce_scatter | solution.py:29
  135.1 190.8 %copy-start.2 = (f32[32,3328]{1,0:T(8,128)S(1)}, f32[32,3328]{1,0:T(8,128)}, u32[]{:S(2)}) copy-start(f32[32,3328]{1,0:T(8,128)} %param.11) | copy-start | bytes 1277956
  135.1 190.8 %copy-start.3 = (f32[32,3328]{1,0:T(8,128)S(1)}, f32[32,3328]{1,0:T(8,128)}, u32[]{:S(2)}) copy-start(f32[32,3328]{1,0:T(8,128)} %param.10) | copy-start | bytes 1277956
  135.2 165.2 %reduce-scatter.6.cloned.1.call-start = ((), (), s32[]{:S(2)}) async-start(), calls=%async_computation.8 | async-start | bytes 4259840 | tf_op jit(solution)/shard_map/reduce_scatter | solution.py:29
  255.1 70.8 %reduce-scatter.8.cloned.1.call-start = ((), (), s32[]{:S(2)}) async-start(), calls=%async_computation.9 | async-start | bytes 1277952 | tf_op jit(solution)/shard_map/reduce_scatter | solution.py:29
  331.7 7.4 %copy-start.1 = (bf16[512,128]{1,0:T(8,128)(2,1)S(1)}, bf16[512,128]{1,0:T(8,128)(2,1)}, u32[]{:S(2)}) copy-start(bf16[512,128]{1,0:T(8,128)(2,1)} %param.7) | copy-start | bytes 393220
  331.7 141.1 %all-to-all-start.2 = ((bf16[32,32,3328]{2,1,0:T(8,128)(2,1)}), bf16[32,32,3328]{2,1,0:T(8,128)(2,1)}, u32[]{:S(2)}, u32[]{:S(2)}) async-start(bf16[32,32,3328]{2,1,0:T(8,128)(2,1)} %stack.2), calls=%async_computation.5 | async-start | bytes 13631488 | tf_op jit(solution)/shard_map/all_to_all | solution.py:69
  339.1 131.9 %all-gather.6.cloned.1.call-start = ((), (), s32[]{:S(2)}) async-start(), calls=%async_computation.10 | async-start | bytes 1572864 | tf_op jit(solution)/shard_map/all_gather | solution.py:36
Sparse Core Ops, SparseCore 0:
  23.4 67.9 all-gather.3
  135.3 119.7 reduce-scatter.3
  257.6 42.6 reduce-scatter.5
  302.7 23.1 reduce-scatter.7
Sparse Core Ops, SparseCore 1:
  448.1 22.8 all-gather.5
